TPU v7x, 32 devices: a whole 2x2x4 slice. The times are simulated.
32 devices in a mesh: expert: 16 (over z, y, x), dp: 2 (over core).
Axes of the slice: x: 2, y: 2, z: 4, core: 2. Of those that a mesh axis runs over, the one named last changes fastest.
Arguments:
- tokens: bfloat16 [2, 256, 4096], P(None, ('expert', 'dp')), may hold values from -6 to 6
- norm_gain: float32 [4096], replicated, may hold values from 0.5 to 1.5
- route_ids: int32 [2, 256, 8], P(None, ('expert', 'dp')), may hold values from 0 to 15, all different within a row; in each aligned block of 8 rows (0 to 7, 8 to 15, ..., all dimensions but the last counted through in order) at most 8 rows name the same one
- route_weights: float32 [2, 256, 8], P(None, ('expert', 'dp')), may hold values from 0.05 to 0.25
- rows_left: int32 [256], P(('expert', 'dp')), may hold values from 1 to 40
- gate_up_elems: bfloat16 [16, 2, 4096, 1024], P('expert', None, None, 'dp'), may hold values from -0.09375 to 0.09375
- gate_up_scales: bfloat16 [16, 2, 128, 1024], P('expert', None, None, 'dp'), may hold values from 0.5 to 2, as said below
- down_elems: bfloat16 [16, 1024, 4096], P('expert', 'dp'), may hold values from -0.1875 to 0.1875
- down_scales: bfloat16 [16, 32, 4096], P('expert', 'dp'), may hold values from 0.5 to 2, as said below
- swap_pairs: int32 [8], replicated, may hold values 0 or 1
Outputs:
- mixed: bfloat16 [2, 256, 4096], P(None, ('expert', 'dp'))
- new_gate_up_elems: bfloat16 [16, 2, 4096, 1024], P('expert', None, None, 'dp')
- new_gate_up_scales: bfloat16 [16, 2, 128, 1024], P('expert', None, None, 'dp')
- new_down_elems: bfloat16 [16, 1024, 4096], P('expert', 'dp')
- new_down_scales: bfloat16 [16, 32, 4096], P('expert', 'dp')
Inputs may be any that keep to these rules, and one draw needn't show every extreme that they name: `route_ids`: within a step each row names 8 different experts; among the 8 rows of one device in a step, at most 8 name any one expert, and exactly 8 do for some expert. `gate_up_scales`: every entry is a power of two. `down_scales`: every entry is a power of two.
All inputs are finite; a program needn't handle non-finite values.
Results may differ from a plain program's by a relative error of at most 0.0077.
Values may be sent and summed in bfloat16 or wider, within the bound.
No kernel may reach another device: no remote copies, remote signals or barrier semaphores. Data moves between devices by JAX's collectives and lax.ppermute only.
A program may use at most 128 MiB of HBM per device.

v0:
```python
import jax
import jax.numpy as jnp
from jax import lax
from jax.sharding import PartitionSpec as P

mx_block = 32


def partner(x, axis, distance):
    return lax.ppermute(x, axis, [(i, i ^ 1 << distance) for i in range(lax.axis_size(axis))])


def dequantize(elems, scales, axis):
    return elems * jnp.repeat(scales, mx_block, axis=axis)


def rms_normed(rows, norm_gain):
    values = rows.astype(jnp.float32)
    factor = lax.rsqrt(jnp.mean(values * values, axis=-1, keepdims=True) + 1e-06)
    return (values * factor * norm_gain).astype(jnp.bfloat16)


def expert_hidden(rows, gate_up):
    both = jnp.einsum("rd,gdf->grf", rows, gate_up, preferred_element_type=jnp.float32)
    return (jax.nn.silu(both[0]) * both[1]).astype(jnp.bfloat16)


def on_device(
    tokens,
    norm_gain,
    route_ids,
    route_weights,
    rows_left,
    gate_up_elems,
    gate_up_scales,
    down_elems,
    down_scales,
    swap_pairs,
):
    slots = lax.axis_size("expert")
    half = slots // 2
    steps, rows, width = tokens.shape
    top = route_ids.shape[2]
    cap = max(2, min(rows, 2 * rows * top // slots))
    here = lax.axis_index("expert")
    pair_iota = jnp.arange(half, dtype=jnp.int32)
    slot_iota = jnp.arange(slots, dtype=jnp.int32)
    own_flag = jnp.sum(jnp.where(pair_iota == here % half, swap_pairs, 0))
    initial = (gate_up_elems, gate_up_scales, down_elems, down_scales)
    swapped = initial
    results = []
    for step in range(steps):
        if step == steps // 2:
            received = partner(
                (gate_up_elems, gate_up_scales, down_elems, down_scales),
                "expert",
                slots.bit_length() - 2,
            )
            swapped = tuple(
                (jnp.where(own_flag > 0, other, mine) for mine, other in zip(initial, received))
            )
        ids = route_ids[step]
        normed = rms_normed(tokens[step], norm_gain)
        live = rows_left > step
        flat_live = jnp.repeat(live, top)
        flat_dest = ids.reshape(-1)
        hits = ((flat_dest[:, None] == slot_iota[None, :]) & flat_live[:, None]).astype(jnp.int32)
        rank = jnp.sum(jnp.cumsum(hits, axis=0) * hits, axis=1) - 1
        slot_index = jnp.where(flat_live, flat_dest * cap + rank, slots * cap)
        sources = jnp.repeat(normed, top, axis=0)
        send = (
            jnp.zeros((slots * cap, width), jnp.bfloat16)
            .at[slot_index]
            .set(sources, mode="drop")
            .reshape(slots, cap, width)
        )
        gate_up = dequantize(initial[0][0], initial[1][0], 1)
        down = dequantize(initial[2][0], initial[3][0], 0)
        arrived = lax.all_to_all(send, "expert", split_axis=0, concat_axis=0, tiled=True)
        piece = lax.all_gather(arrived, "dp", axis=0, tiled=True)
        flat = piece.reshape(-1, width)
        hidden = expert_hidden(flat, gate_up).reshape(piece.shape[0], piece.shape[1], -1)
        hidden_rows = hidden.reshape(-1, hidden.shape[2])
        summed = lax.psum_scatter(
            jnp.dot(hidden_rows, down, preferred_element_type=jnp.float32).astype(jnp.bfloat16),
            "dp",
            scatter_dimension=0,
            tiled=True,
        )
        result = summed.reshape(slots, cap, width)
        back = lax.all_to_all(result, "expert", split_axis=0, concat_axis=0, tiled=True)
        picked = back.reshape(-1, width)[jnp.minimum(slot_index, slots * cap - 1)]
        factor = route_weights[step].reshape(-1) * flat_live.astype(jnp.float32)
        mixed_step = jnp.sum(
            (picked.astype(jnp.float32) * factor[:, None]).reshape(rows, top, width), axis=1
        )
        results.append(mixed_step.astype(jnp.bfloat16))
    mixed = jnp.stack(results)
    return (mixed, swapped[0], swapped[1], swapped[2], swapped[3])


def solution(mesh):
    in_specs = (
        P(None, ("expert", "dp"), None),
        P(),
        P(None, ("expert", "dp"), None),
        P(None, ("expert", "dp"), None),
        P(("expert", "dp")),
        P("expert", None, None, "dp"),
        P("expert", None, None, "dp"),
        P("expert", "dp", None),
        P("expert", "dp", None),
        P(),
    )
    out_specs = (
        P(None, ("expert", "dp"), None),
        P("expert", None, None, "dp"),
        P("expert", None, None, "dp"),
        P("expert", "dp", None),
        P("expert", "dp", None),
    )
    return jax.shard_map(
        on_device, mesh=mesh, in_specs=in_specs, out_specs=out_specs, check_vma=False
    )
```

profile of v0, /device:TPU:17, one launch (start us, length us, event | category | flops | bytes accessed | tf_op | source)
XLA Modules:
  0.0 702.7 jit_solution(17926109491885856133)
XLA Ops:
  8.1 0.7 fusion.57
  9.4 1.0 fusion.36
  10.4 1.0 fusion.38
  11.4 2.4 scatter_custom_fusion
  13.8 6.6 all-to-all-start
  21.4 112.9 %all-to-all-done = bf16[16,8,4096]{2,1,0:T(8,128)(2,1)S(1)} async-done(((bf16[16,8,4096]{2,1,0:T(8,128)(2,1)}), bf16[16,8,4096]{2,1,0:T(8,128)(2,1)S(1)}, u32[]{:S(2)}, u32[]{:S(2)}) %all-to-all-start) | async-done | bytes 1048608 | tf_op jit(solution)/shard_map/all_to_all | solution.py:79
  134.3 1.0 copy-done.1
  135.3 2.4 scatter_custom_fusion.1
  137.7 4.8 all-to-all-start.2
  143.9 102.8 %all-to-all-done.2 = bf16[16,8,4096]{2,1,0:T(8,128)(2,1)S(1)} async-done(((bf16[16,8,4096]{2,1,0:T(8,128)(2,1)}), bf16[16,8,4096]{2,1,0:T(8,128)(2,1)S(1)}, u32[]{:S(2)}, u32[]{:S(2)}) %all-to-all-start.2) | async-done | bytes 1048608 | tf_op jit(solution)/shard_map/all_to_all | solution.py:79
  246.7 1.0 copy-done.2
  247.8 0.7 broadcast_in_dim.19
  248.5 0.9 copy-done.9
  249.4 8.1 %fusion.10 = f32[2,256,512]{1,2,0:T(8,128)S(1)} fusion(bf16[32,8,4096]{2,1,0:T(8,128)(2,1)S(1)} %copy-done.9, bf16[1,2,4096,512]{3,2,1,0:T(8,128)(2,1)} %param.15, bf16[1,2,4096,512]{3,2,1,0:T(8,128)(2,1)S(1)} %bitcast.100), kind=kOutput, calls=%fused_computation.19 | convolution fusion | flops 2151677952 | bytes 19922944 | tf_op jit(solution)/shard_map/rd,gdf->grf/dot_general | solution.py:24
  258.0 1.9 copy-done.3
  260.0 2.5 broadcast_select_fusion.1
  262.5 2.0 copy-done.4
  264.4 2.7 convolution_convert_fusion.1
  267.5 9.0 %fusion.15 = f32[2,256,512]{1,2,0:T(8,128)S(1)} fusion(bf16[32,8,4096]{2,1,0:T(8,128)(2,1)} %all-gather.5.cloned.1.call-done, bf16[1,2,4096,512]{3,2,1,0:T(8,128)(2,1)} %param.15, bf16[1,2,4096,512]{3,2,1,0:T(8,128)(2,1)} %bitcast.101), kind=kOutput, calls=%fused_computation.20 | convolution fusion | flops 2151677952 | bytes 19922944 | tf_op jit(solution)/shard_map/rd,gdf->grf/dot_general | solution.py:24
  276.6 2.7 convolution_convert_fusion
  279.3 0.8 reduce-scatter.3.cloned.1.call-done
  280.1 7.7 %all-to-all-start.1 = ((bf16[16,8,4096]{2,1,0:T(8,128)(2,1)}), bf16[16,8,4096]{2,1,0:T(8,128)(2,1)S(1)}, u32[]{:S(2)}, u32[]{:S(2)}) async-start(bf16[16,8,4096]{2,1,0:T(8,128)(2,1)} %bitcast.103), calls=%async_computation.2 | async-start | bytes 2097152 | tf_op jit(solution)/shard_map/all_to_all | solution.py:91
  287.9 2.2 collective-permute-start.3
  290.2 4.7 reduce-scatter.5.cloned.1.call-done
  294.9 367.7 %all-to-all-done.1 = bf16[16,8,4096]{2,1,0:T(8,128)(2,1)S(1)} async-done(((bf16[16,8,4096]{2,1,0:T(8,128)(2,1)}), bf16[16,8,4096]{2,1,0:T(8,128)(2,1)S(1)}, u32[]{:S(2)}, u32[]{:S(2)}) %all-to-all-start.1) | async-done | bytes 1048608 | tf_op jit(solution)/shard_map/all_to_all | solution.py:91
  662.7 4.9 all-to-all-start.3
  667.6 0.7 broadcast_select_fusion.3
  668.2 0.7 broadcast_select_fusion.2
  669.0 7.3 %broadcast_select_fusion = bf16[1,2,4096,512]{3,2,1,0:T(8,128)(2,1)} fusion(bf16[1,2,4096,512]{3,2,1,0:T(8,128)(2,1)} %collective-permute-done, bf16[1,2,4096,512]{3,2,1,0:T(8,128)(2,1)} %param.15, pred[]{:T(512)S(6)} %gt.14), kind=kLoop, calls=%fused_computation.8 | loop fusion | flops 4194304 | bytes 25165824 | tf_op jit(solution)/shard_map/jit(_where)/select_n | solution.py:60
  676.2 0.9 gather_fusion
  677.6 16.6 %all-to-all-done.3 = bf16[16,8,4096]{2,1,0:T(8,128)(2,1)S(1)} async-done(((bf16[16,8,4096]{2,1,0:T(8,128)(2,1)}), bf16[16,8,4096]{2,1,0:T(8,128)(2,1)S(1)}, u32[]{:S(2)}, u32[]{:S(2)}) %all-to-all-start.3) | async-done | bytes 1048608 | tf_op jit(solution)/shard_map/all_to_all | solution.py:91
  694.1 0.9 gather_fusion.1
  (64 shorter events, 5.9 us)
Async XLA Ops:
  7.2 135.4 %copy-start.10 = (s32[8]{0:T(128)S(1)}, s32[8]{0:T(128)}, u32[]{:S(2)}) copy-start(s32[8]{0:T(128)} %param.19) | copy-start | bytes 100
  11.4 236.4 %copy-start.6 = (bf16[1,2,128,512]{3,2,1,0:T(8,128)(2,1)S(1)}, bf16[1,2,128,512]{3,2,1,0:T(8,128)(2,1)}, u32[]{:S(2)}) copy-start(bf16[1,2,128,512]{3,2,1,0:T(8,128)(2,1)} %param.16) | copy-start | bytes 786436
  13.8 120.4 %all-to-all-start = ((bf16[16,8,4096]{2,1,0:T(8,128)(2,1)}), bf16[16,8,4096]{2,1,0:T(8,128)(2,1)S(1)}, u32[]{:S(2)}, u32[]{:S(2)}) async-start(bf16[16,8,4096]{2,1,0:T(8,128)(2,1)} %bitcast.8), calls=%async_computation | async-start | bytes 2097152 | tf_op jit(solution)/shard_map/all_to_all | solution.py:79
  20.4 227.4 %all-gather.3.cloned.1.call-start = ((), (), s32[]{:S(2)}) async-start(), calls=%async_computation.6 | async-start | bytes 3145728 | tf_op jit(solution)/shard_map/all_gather | solution.py:80
  20.4 237.1 %collective-permute-start.2 = (bf16[1,512,4096]{2,1,0:T(8,128)(2,1)}, bf16[1,512,4096]{2,1,0:T(8,128)(2,1)}, u32[]{:S(2)}, u32[]{:S(2)}) collective-permute-start(bf16[1,512,4096]{2,1,0:T(8,128)(2,1)} %param.17), channel_id=1, source_target_pairs={{0,16},{2,18},{4,20},{6,22},{8,24},{10,26},{12,28},{14,30},{16,0},... | collective-permute-start | bytes 12582920 | tf_op jit(solution)/shard_map/ppermute | solution.py:10
  134.3 1.0 copy-start.1
  137.7 109.0 %all-to-all-start.2 = ((bf16[16,8,4096]{2,1,0:T(8,128)(2,1)}), bf16[16,8,4096]{2,1,0:T(8,128)(2,1)S(1)}, u32[]{:S(2)}, u32[]{:S(2)}) async-start(bf16[16,8,4096]{2,1,0:T(8,128)(2,1)} %bitcast.27), calls=%async_computation.3 | async-start | bytes 2097152 | tf_op jit(solution)/shard_map/all_to_all | solution.py:79
  142.5 124.9 %all-gather.5.cloned.1.call-start = ((), (), s32[]{:S(2)}) async-start(), calls=%async_computation.8 | async-start | bytes 3145728 | tf_op jit(solution)/shard_map/all_gather | solution.py:80
  246.7 1.0 copy-start.2
  247.7 32.4 %reduce-scatter.3.cloned.1.call-start = ((), (), s32[]{:S(2)}) async-start(), calls=%async_computation.7 | async-start | bytes 3145728 | tf_op jit(solution)/shard_map/reduce_scatter | solution.py:84
  247.8 1.6 copy-start.9
  248.5 9.0 %copy-start = (bf16[2,128,32,512]{3,2,1,0:T(8,128)(2,1)}, bf16[2,128,32,512]{3,2,1,0:T(8,128)(2,1)S(1)}, u32[]{:S(2)}) copy-start(bf16[2,128,32,512]{3,2,1,0:T(8,128)(2,1)S(1)} %broadcast_in_dim.19) | copy-start | bytes 25165828
  249.4 8.1 %copy-start.7 = (bf16[1,16,4096]{2,1,0:T(8,128)(2,1)S(1)}, bf16[1,16,4096]{2,1,0:T(8,128)(2,1)}, u32[]{:S(2)}) copy-start(bf16[1,16,4096]{2,1,0:T(8,128)(2,1)} %param.18) | copy-start | bytes 393220
  257.5 2.5 copy-start.3
  262.5 2.0 copy-start.4
  267.1 27.8 %reduce-scatter.5.cloned.1.call-start = ((), (), s32[]{:S(2)}) async-start(), calls=%async_computation.9 | async-start | bytes 3145728 | tf_op jit(solution)/shard_map/reduce_scatter | solution.py:84
  267.4 401.6 %collective-permute-start = (bf16[1,2,4096,512]{3,2,1,0:T(8,128)(2,1)}, bf16[1,2,4096,512]{3,2,1,0:T(8,128)(2,1)}, u32[]{:S(2)}, u32[]{:S(2)}) collective-permute-start(bf16[1,2,4096,512]{3,2,1,0:T(8,128)(2,1)} %param.15), channel_id=1, source_target_pairs={{0,16},{2,18},{4,20},{6,22},{8,24},{10,26},{12,28},{14,30},{16,0},... | collective-permute-start | bytes 25165832 | tf_op jit(solution)/shard_map/ppermute | solution.py:10
  267.5 9.1 %copy-start.5 = (bf16[1,512,4096]{2,1,0:T(8,128)(2,1)S(1)}, bf16[1,512,4096]{2,1,0:T(8,128)(2,1)}, u32[]{:S(2)}) copy-start(bf16[1,512,4096]{2,1,0:T(8,128)(2,1)} %copy-done.4) | copy-start | bytes 12582916
  276.5 13.6 %copy-start.8 = (f32[2,8,8]{2,1,0:T(8,128)S(1)}, f32[2,8,8]{2,1,0:T(8,128)}, u32[]{:S(2)}) copy-start(f32[2,8,8]{2,1,0:T(8,128)} %param.13) | copy-start | bytes 1540
  280.1 382.6 %all-to-all-start.1 = ((bf16[16,8,4096]{2,1,0:T(8,128)(2,1)}), bf16[16,8,4096]{2,1,0:T(8,128)(2,1)S(1)}, u32[]{:S(2)}, u32[]{:S(2)}) async-start(bf16[16,8,4096]{2,1,0:T(8,128)(2,1)} %bitcast.103), calls=%async_computation.2 | async-start | bytes 2097152 | tf_op jit(solution)/shard_map/all_to_all | solution.py:91
  287.8 380.4 %collective-permute-start.1 = (bf16[1,2,128,512]{3,2,1,0:T(8,128)(2,1)S(1)}, bf16[1,2,128,512]{3,2,1,0:T(8,128)(2,1)S(1)}, u32[]{:S(2)}, u32[]{:S(2)}) collective-permute-start(bf16[1,2,128,512]{3,2,1,0:T(8,128)(2,1)S(1)} %copy-done.6), channel_id=1, source_target_pairs={{0,16},{2,18},{4,20},{6,22},{8,24},{10,26},{12,28},{14,30},{16,0},... | collective-permute-start | bytes 786440 | tf_op jit(solution)/shard_map/ppermute | solution.py:10
  287.9 379.6 %collective-permute-start.3 = (bf16[1,16,4096]{2,1,0:T(8,128)(2,1)S(1)}, bf16[1,16,4096]{2,1,0:T(8,128)(2,1)S(1)}, u32[]{:S(2)}, u32[]{:S(2)}) collective-permute-start(bf16[1,16,4096]{2,1,0:T(8,128)(2,1)S(1)} %copy-done.7), channel_id=1, source_target_pairs={{0,16},{2,18},{4,20},{6,22},{8,24},{10,26},{12,28},{14,30},{16,0},... | collective-permute-start | bytes 393224 | tf_op jit(solution)/shard_map/ppermute | solution.py:10
  662.7 31.5 %all-to-all-start.3 = ((bf16[16,8,4096]{2,1,0:T(8,128)(2,1)}), bf16[16,8,4096]{2,1,0:T(8,128)(2,1)S(1)}, u32[]{:S(2)}, u32[]{:S(2)}) async-start(bf16[16,8,4096]{2,1,0:T(8,128)(2,1)} %bitcast.102), calls=%async_computation.5 | async-start | bytes 2097152 | tf_op jit(solution)/shard_map/all_to_all | solution.py:91
Sparse Core Ops, SparseCore 0:
  135.4 13.4 all-gather.2
  247.8 12.0 all-gather.4
  267.2 12.7 reduce-scatter.2
  282.7 12.1 reduce-scatter.4
where the time goes:
time: 703 us
  waiting for transfers between devices  606 us (86%)
  starting transfers between devices  26.9 us (4%)
  matrix products  22.5 us (3%)
  other arithmetic  17.6 us (3%)
  local copies, waits for them, and re-layouts  15.3 us (2%)
  between operations  14.7 us (2%)
    all_to_all x2, waiting for transfers between devices, on_device(): lax.all_to_all(result, 'expert', split_axis=0, concat_axis=0, tiled=True)  384 us
    all_to_all x2, waiting for transfers between devices, on_device(): lax.all_to_all(send, 'expert', split_axis=0, concat_axis=0, tiled=True)  216 us
    dot_general x2, matrix products, expert_hidden(): jnp.einsum('rd,gdf->grf', rows, gate_up, preferred_element_type=jnp.float32)  17.1 us
  transfers between devices with their start and end apart: 12, of which 6 were waited for; matrix products, arithmetic and copies ran while one was open for 6% of the time, Pallas kernels for 0%

commit v1 on v0

--- a/solution.py
+++ b/solution.py
@@ -88,7 +88,17 @@
             tiled=True,
         )
         result = summed.reshape(slots, cap, width)
-        back = lax.all_to_all(result, "expert", split_axis=0, concat_axis=0, tiled=True)
+        after, before = (lax.axis_size("expert"), lax.axis_index("expert"))
+        near = result.shape[0] // after
+        block_out = jnp.roll(result, shift=-before * near, axis=0)
+        so_far_all = [lax.slice_in_dim(block_out, 0, near, axis=0)]
+        for k0 in range(1, after):
+            block_now = lax.slice_in_dim(block_out, k0 * near, (k0 + 1) * near, axis=0)
+            so_far_all.append(
+                lax.ppermute(block_now, "expert", [(m, (m + k0) % after) for m in range(after)])
+            )
+        prior = jnp.concatenate(so_far_all[::-1], axis=0)
+        back = jnp.roll(prior, shift=(before + 1) * so_far_all[0].shape[0], axis=0)
         picked = back.reshape(-1, width)[jnp.minimum(slot_index, slots * cap - 1)]
         factor = route_weights[step].reshape(-1) * flat_live.astype(jnp.float32)
         mixed_step = jnp.sum(

time: 703 us -> 738 us (1.050)
  starting transfers between devices: 26.9 us -> 68.3 us
  waiting for transfers between devices: 606 us -> 589 us
    all_to_all x2 -> x0, waiting for transfers between devices: 384 us -> none  [on_device(): lax.all_to_all(result, 'expert', split_axis=0, concat_axis=0, tiled=True)]
    ppermute x4, waiting for transfers between devices: 0.01 us -> 361 us  [partner(): lax.ppermute(x, axis, [(i, i ^ 1 << distance) for i in range(lax.axis_siz...]
    ppermute x0 -> x30, starting transfers between devices: none -> 53.9 us  [on_device(): lax.ppermute(block_now, 'expert', [(m, (m + k0) % after) for m in range(a...]
    all_to_all x2 -> x0, starting transfers between devices: 12.6 us -> none  [on_device(): lax.all_to_all(result, 'expert', split_axis=0, concat_axis=0, tiled=True)]
    ppermute x0 -> x30, waiting for transfers between devices: none -> 11.7 us  [on_device(): lax.ppermute(block_now, 'expert', [(m, (m + k0) % after) for m in range(a...]
  transfers between devices with their start and end apart: 12 -> 40, of which waited for: 6 -> 9; matrix products, arithmetic and copies ran while one was open for 6% -> 6% of each run, Pallas kernels for 0% -> 0%
where the time goes in v1:
time: 738 us; the launch traced here: 732 us
  waiting for transfers between devices  589 us (80%)
  starting transfers between devices  68.3 us (9%)
  matrix products  22.5 us (3%)
  other arithmetic  21.5 us (3%)
  local copies, waits for them, and re-layouts  15.6 us (2%)
  between operations  14.9 us (2%)
    ppermute x4, waiting for transfers between devices, partner(): lax.ppermute(x, axis, [(i, i ^ 1 << distance) for i in range(lax.axis_siz...  361 us
    all_to_all x2, waiting for transfers between devices, on_device(): lax.all_to_all(send, 'expert', split_axis=0, concat_axis=0, tiled=True)  217 us
    ppermute x30, starting transfers between devices, on_device(): lax.ppermute(block_now, 'expert', [(m, (m + k0) % after) for m in range(a...  53.9 us
    dot_general x2, matrix products, expert_hidden(): jnp.einsum('rd,gdf->grf', rows, gate_up, preferred_element_type=jnp.float32)  17.2 us
  transfers between devices with their start and end apart: 40, of which 9 were waited for; matrix products, arithmetic and copies ran while one was open for 6% of the time, Pallas kernels for 0%

profile of v1, /device:TPU:17, one launch (start us, length us, event | category | flops | bytes accessed | tf_op | source)
XLA Modules:
  0.0 731.9 jit_solution(5793999605969523999)
XLA Ops:
  12.3 2.4 scatter_custom_fusion
  14.6 6.6 all-to-all-start
  21.4 113.7 %all-to-all-done = bf16[16,8,4096]{2,1,0:T(8,128)(2,1)S(1)} async-done(((bf16[16,8,4096]{2,1,0:T(8,128)(2,1)}), bf16[16,8,4096]{2,1,0:T(8,128)(2,1)S(1)}, u32[]{:S(2)}, u32[]{:S(2)}) %all-to-all-start) | async-done | bytes 1048608 | tf_op jit(solution)/shard_map/all_to_all | solution.py:79
  136.1 2.4 scatter_custom_fusion.1
  138.5 4.8 all-to-all-start.1
  144.7 102.8 %all-to-all-done.1 = bf16[16,8,4096]{2,1,0:T(8,128)(2,1)S(1)} async-done(((bf16[16,8,4096]{2,1,0:T(8,128)(2,1)}), bf16[16,8,4096]{2,1,0:T(8,128)(2,1)S(1)}, u32[]{:S(2)}, u32[]{:S(2)}) %all-to-all-start.1) | async-done | bytes 1048608 | tf_op jit(solution)/shard_map/all_to_all | solution.py:79
  250.2 8.1 %fusion.10 = f32[2,256,512]{1,2,0:T(8,128)S(1)} fusion(bf16[32,8,4096]{2,1,0:T(8,128)(2,1)S(1)} %copy-done.9, bf16[1,2,4096,512]{3,2,1,0:T(8,128)(2,1)} %param.17, bf16[1,2,4096,512]{3,2,1,0:T(8,128)(2,1)S(1)} %bitcast.100), kind=kOutput, calls=%fused_computation.27 | convolution fusion | flops 2151677952 | bytes 19922944 | tf_op jit(solution)/shard_map/rd,gdf->grf/dot_general | solution.py:24
  258.9 1.9 copy-done.3
  260.8 2.4 broadcast_select_fusion.1
  263.2 2.0 copy-done.4
  265.2 2.6 convolution_convert_fusion.1
  268.2 9.0 %fusion.15 = f32[2,256,512]{1,2,0:T(8,128)S(1)} fusion(bf16[32,8,4096]{2,1,0:T(8,128)(2,1)} %all-gather.5.cloned.1.call-done, bf16[1,2,4096,512]{3,2,1,0:T(8,128)(2,1)} %param.17, bf16[1,2,4096,512]{3,2,1,0:T(8,128)(2,1)} %bitcast.101), kind=kOutput, calls=%fused_computation.28 | convolution fusion | flops 2151677952 | bytes 19922944 | tf_op jit(solution)/shard_map/rd,gdf->grf/dot_general | solution.py:24
  277.2 2.7 convolution_convert_fusion
  280.0 2.4 collective-permute-start.31
  282.5 360.7 %collective-permute-done.33 = bf16[1,16,4096]{2,1,0:T(8,128)(2,1)S(1)} collective-permute-done((bf16[1,16,4096]{2,1,0:T(8,128)(2,1)S(1)}, bf16[1,16,4096]{2,1,0:T(8,128)(2,1)S(1)}, u32[]{:S(2)}, u32[]{:S(2)}) %collective-permute-start.33) | collective-permute-done | bytes 131104 | tf_op jit(solution)/shard_map/ppermute | solution.py:10
  646.4 4.7 collective-permute-start
  652.2 5.1 collective-permute-start.3
  659.6 7.3 broadcast_select_fusion
  667.0 2.6 collective-permute-start.6
  669.9 3.3 collective-permute-start.8
  673.8 2.6 collective-permute-start.10
  677.2 3.5 collective-permute-start.12
  680.8 1.7 collective-permute-start.13
  682.5 2.9 collective-permute-start.14
  685.4 1.7 collective-permute-start.15
  689.0 4.6 collective-permute-start.18
  693.7 3.0 collective-permute-start.19
  699.4 3.2 collective-permute-start.23
  703.6 2.4 collective-permute-start.25
  707.3 4.1 collective-permute-done.22
  711.5 4.8 collective-permute-start.28
  718.2 3.0 collective-permute-done.29
  (156 shorter events, 31.9 us)
Async XLA Ops:
  14.6 120.4 %all-to-all-start = ((bf16[16,8,4096]{2,1,0:T(8,128)(2,1)}), bf16[16,8,4096]{2,1,0:T(8,128)(2,1)S(1)}, u32[]{:S(2)}, u32[]{:S(2)}) async-start(bf16[16,8,4096]{2,1,0:T(8,128)(2,1)} %bitcast.8), calls=%async_computation | async-start | bytes 2097152 | tf_op jit(solution)/shard_map/all_to_all | solution.py:79
  21.2 227.4 %all-gather.3.cloned.1.call-start = ((), (), s32[]{:S(2)}) async-start(), calls=%async_computation.4 | async-start | bytes 3145728 | tf_op jit(solution)/shard_map/all_gather | solution.py:80
  21.2 237.1 %collective-permute-start.32 = (bf16[1,512,4096]{2,1,0:T(8,128)(2,1)}, bf16[1,512,4096]{2,1,0:T(8,128)(2,1)}, u32[]{:S(2)}, u32[]{:S(2)}) collective-permute-start(bf16[1,512,4096]{2,1,0:T(8,128)(2,1)} %param.19), channel_id=1, source_target_pairs={{0,16},{2,18},{4,20},{6,22},{8,24},{10,26},{12,28},{14,30},{16,0},... | collective-permute-start | bytes 12582920 | tf_op jit(solution)/shard_map/ppermute | solution.py:10
  138.5 109.0 %all-to-all-start.1 = ((bf16[16,8,4096]{2,1,0:T(8,128)(2,1)}), bf16[16,8,4096]{2,1,0:T(8,128)(2,1)S(1)}, u32[]{:S(2)}, u32[]{:S(2)}) async-start(bf16[16,8,4096]{2,1,0:T(8,128)(2,1)} %bitcast.27), calls=%async_computation.2 | async-start | bytes 2097152 | tf_op jit(solution)/shard_map/all_to_all | solution.py:79
  143.3 124.8 %all-gather.5.cloned.1.call-start = ((), (), s32[]{:S(2)}) async-start(), calls=%async_computation.6 | async-start | bytes 3145728 | tf_op jit(solution)/shard_map/all_gather | solution.py:80
  248.5 396.2 %reduce-scatter.3.cloned.1.call-start = ((), (), s32[]{:S(2)}) async-start(), calls=%async_computation.5 | async-start | bytes 3145728 | tf_op jit(solution)/shard_map/reduce_scatter | solution.py:84
  267.8 389.4 %reduce-scatter.5.cloned.1.call-start = ((), (), s32[]{:S(2)}) async-start(), calls=%async_computation.7 | async-start | bytes 3145728 | tf_op jit(solution)/shard_map/reduce_scatter | solution.py:84
  268.0 390.8 %collective-permute-start.30 = (bf16[1,2,4096,512]{3,2,1,0:T(8,128)(2,1)}, bf16[1,2,4096,512]{3,2,1,0:T(8,128)(2,1)}, u32[]{:S(2)}, u32[]{:S(2)}) collective-permute-start(bf16[1,2,4096,512]{3,2,1,0:T(8,128)(2,1)} %param.17), channel_id=1, source_target_pairs={{0,16},{2,18},{4,20},{6,22},{8,24},{10,26},{12,28},{14,30},{16,0},... | collective-permute-start | bytes 25165832 | tf_op jit(solution)/shard_map/ppermute | solution.py:10
  280.0 364.0 %collective-permute-start.31 = (bf16[1,2,128,512]{3,2,1,0:T(8,128)(2,1)S(1)}, bf16[1,2,128,512]{3,2,1,0:T(8,128)(2,1)S(1)}, u32[]{:S(2)}, u32[]{:S(2)}) collective-permute-start(bf16[1,2,128,512]{3,2,1,0:T(8,128)(2,1)S(1)} %copy-done.6), channel_id=1, source_target_pairs={{0,16},{2,18},{4,20},{6,22},{8,24},{10,26},{12,28},{14,30},{16,0},... | collective-permute-start | bytes 786440 | tf_op jit(solution)/shard_map/ppermute | solution.py:10
  282.4 360.9 %collective-permute-start.33 = (bf16[1,16,4096]{2,1,0:T(8,128)(2,1)S(1)}, bf16[1,16,4096]{2,1,0:T(8,128)(2,1)S(1)}, u32[]{:S(2)}, u32[]{:S(2)}) collective-permute-start(bf16[1,16,4096]{2,1,0:T(8,128)(2,1)S(1)} %copy-done.7), channel_id=1, source_target_pairs={{0,16},{2,18},{4,20},{6,22},{8,24},{10,26},{12,28},{14,30},{16,0},... | collective-permute-start | bytes 393224 | tf_op jit(solution)/shard_map/ppermute | solution.py:10
  646.4 20.5 %collective-permute-start = (bf16[1,8,4096]{2,1,0:T(8,128)(2,1)S(1)}, bf16[1,8,4096]{2,1,0:T(8,128)(2,1)S(1)}, u32[]{:S(2)}, u32[]{:S(2)}) collective-permute-start(bf16[1,8,4096]{2,1,0:T(8,128)(2,1)S(1)} %get-tuple-element.28), channel_id=1, source_target_pairs={{0,30},{2,0},{4,2},{6,4},{8,6},{10,8},{12,10},{14,12},{16,14},{18,... | collective-permute-start | bytes 196616 | tf_op jit(solution)/shard_map/ppermute | solution.py:98
  651.0 15.9 %collective-permute-start.1 = (bf16[1,8,4096]{2,1,0:T(8,128)(2,1)S(1)}, bf16[1,8,4096]{2,1,0:T(8,128)(2,1)S(1)}, u32[]{:S(2)}, u32[]{:S(2)}) collective-permute-start(bf16[1,8,4096]{2,1,0:T(8,128)(2,1)S(1)} %get-tuple-element.27), channel_id=1, source_target_pairs={{0,28},{2,30},{4,0},{6,2},{8,4},{10,6},{12,8},{14,10},{16,12},{18,... | collective-permute-start | bytes 196616 | tf_op jit(solution)/shard_map/ppermute | solution.py:98
  651.8 17.8 %collective-permute-start.2 = (bf16[1,8,4096]{2,1,0:T(8,128)(2,1)S(1)}, bf16[1,8,4096]{2,1,0:T(8,128)(2,1)S(1)}, u32[]{:S(2)}, u32[]{:S(2)}) collective-permute-start(bf16[1,8,4096]{2,1,0:T(8,128)(2,1)S(1)} %get-tuple-element.26), channel_id=1, source_target_pairs={{0,26},{2,28},{4,30},{6,0},{8,2},{10,4},{12,6},{14,8},{16,10},{18,... | collective-permute-start | bytes 196616 | tf_op jit(solution)/shard_map/ppermute | solution.py:98
  652.2 17.8 %collective-permute-start.3 = (bf16[1,8,4096]{2,1,0:T(8,128)(2,1)S(1)}, bf16[1,8,4096]{2,1,0:T(8,128)(2,1)S(1)}, u32[]{:S(2)}, u32[]{:S(2)}) collective-permute-start(bf16[1,8,4096]{2,1,0:T(8,128)(2,1)S(1)} %get-tuple-element.25), channel_id=1, source_target_pairs={{0,24},{2,26},{4,28},{6,30},{8,0},{10,2},{12,4},{14,6},{16,8},{18,... | collective-permute-start | bytes 196616 | tf_op jit(solution)/shard_map/ppermute | solution.py:98
  658.8 14.4 %collective-permute-start.4 = (bf16[1,8,4096]{2,1,0:T(8,128)(2,1)S(1)}, bf16[1,8,4096]{2,1,0:T(8,128)(2,1)S(1)}, u32[]{:S(2)}, u32[]{:S(2)}) collective-permute-start(bf16[1,8,4096]{2,1,0:T(8,128)(2,1)S(1)} %get-tuple-element.24), channel_id=1, source_target_pairs={{0,22},{2,24},{4,26},{6,28},{8,30},{10,0},{12,2},{14,4},{16,6},{18... | collective-permute-start | bytes 196616 | tf_op jit(solution)/shard_map/ppermute | solution.py:98
  667.0 9.5 %collective-permute-start.6 = (bf16[1,8,4096]{2,1,0:T(8,128)(2,1)S(1)}, bf16[1,8,4096]{2,1,0:T(8,128)(2,1)S(1)}, u32[]{:S(2)}, u32[]{:S(2)}) collective-permute-start(bf16[1,8,4096]{2,1,0:T(8,128)(2,1)S(1)} %get-tuple-element.22), channel_id=1, source_target_pairs={{0,18},{2,20},{4,22},{6,24},{8,26},{10,28},{12,30},{14,0},{16,2},{... | collective-permute-start | bytes 196616 | tf_op jit(solution)/shard_map/ppermute | solution.py:98
  669.9 10.9 %collective-permute-start.8 = (bf16[1,8,4096]{2,1,0:T(8,128)(2,1)S(1)}, bf16[1,8,4096]{2,1,0:T(8,128)(2,1)S(1)}, u32[]{:S(2)}, u32[]{:S(2)}) collective-permute-start(bf16[1,8,4096]{2,1,0:T(8,128)(2,1)S(1)} %get-tuple-element.20), channel_id=1, source_target_pairs={{0,14},{2,16},{4,18},{6,20},{8,22},{10,24},{12,26},{14,28},{16,30}... | collective-permute-start | bytes 196616 | tf_op jit(solution)/shard_map/ppermute | solution.py:98
  673.2 9.2 %collective-permute-start.9 = (bf16[1,8,4096]{2,1,0:T(8,128)(2,1)S(1)}, bf16[1,8,4096]{2,1,0:T(8,128)(2,1)S(1)}, u32[]{:S(2)}, u32[]{:S(2)}) collective-permute-start(bf16[1,8,4096]{2,1,0:T(8,128)(2,1)S(1)} %get-tuple-element.19), channel_id=1, source_target_pairs={{0,12},{2,14},{4,16},{6,18},{8,20},{10,22},{12,24},{14,26},{16,28}... | collective-permute-start | bytes 196616 | tf_op jit(solution)/shard_map/ppermute | solution.py:98
  673.8 11.6 %collective-permute-start.10 = (bf16[1,8,4096]{2,1,0:T(8,128)(2,1)S(1)}, bf16[1,8,4096]{2,1,0:T(8,128)(2,1)S(1)}, u32[]{:S(2)}, u32[]{:S(2)}) collective-permute-start(bf16[1,8,4096]{2,1,0:T(8,128)(2,1)S(1)} %get-tuple-element.18), channel_id=1, source_target_pairs={{0,10},{2,12},{4,14},{6,16},{8,18},{10,20},{12,22},{14,24},{16,26}... | collective-permute-start | bytes 196616 | tf_op jit(solution)/shard_map/ppermute | solution.py:98
  676.5 10.6 %collective-permute-start.11 = (bf16[1,8,4096]{2,1,0:T(8,128)(2,1)S(1)}, bf16[1,8,4096]{2,1,0:T(8,128)(2,1)S(1)}, u32[]{:S(2)}, u32[]{:S(2)}) collective-permute-start(bf16[1,8,4096]{2,1,0:T(8,128)(2,1)S(1)} %get-tuple-element.17), channel_id=1, source_target_pairs={{0,8},{2,10},{4,12},{6,14},{8,16},{10,18},{12,20},{14,22},{16,24},... | collective-permute-start | bytes 196616 | tf_op jit(solution)/shard_map/ppermute | solution.py:98
  677.2 10.2 %collective-permute-start.12 = (bf16[1,8,4096]{2,1,0:T(8,128)(2,1)S(1)}, bf16[1,8,4096]{2,1,0:T(8,128)(2,1)S(1)}, u32[]{:S(2)}, u32[]{:S(2)}) collective-permute-start(bf16[1,8,4096]{2,1,0:T(8,128)(2,1)S(1)} %get-tuple-element.16), channel_id=1, source_target_pairs={{0,6},{2,8},{4,10},{6,12},{8,14},{10,16},{12,18},{14,20},{16,22},{... | collective-permute-start | bytes 196616 | tf_op jit(solution)/shard_map/ppermute | solution.py:98
  682.5 11.2 %collective-permute-start.14 = (bf16[1,8,4096]{2,1,0:T(8,128)(2,1)S(1)}, bf16[1,8,4096]{2,1,0:T(8,128)(2,1)S(1)}, u32[]{:S(2)}, u32[]{:S(2)}) collective-permute-start(bf16[1,8,4096]{2,1,0:T(8,128)(2,1)S(1)} %get-tuple-element.14), channel_id=1, source_target_pairs={{0,2},{2,4},{4,6},{6,8},{8,10},{10,12},{12,14},{14,16},{16,18},{18... | collective-permute-start | bytes 196616 | tf_op jit(solution)/shard_map/ppermute | solution.py:98
  685.4 11.3 %collective-permute-start.15 = (bf16[1,8,4096]{2,1,0:T(8,128)(2,1)S(1)}, bf16[1,8,4096]{2,1,0:T(8,128)(2,1)S(1)}, u32[]{:S(2)}, u32[]{:S(2)}) collective-permute-start(bf16[1,8,4096]{2,1,0:T(8,128)(2,1)S(1)} %get-tuple-element.43), channel_id=1, source_target_pairs={{0,30},{2,0},{4,2},{6,4},{8,6},{10,8},{12,10},{14,12},{16,14},{18,... | collective-permute-start | bytes 196616 | tf_op jit(solution)/shard_map/ppermute | solution.py:98
  687.1 9.7 %collective-permute-start.16 = (bf16[1,8,4096]{2,1,0:T(8,128)(2,1)S(1)}, bf16[1,8,4096]{2,1,0:T(8,128)(2,1)S(1)}, u32[]{:S(2)}, u32[]{:S(2)}) collective-permute-start(bf16[1,8,4096]{2,1,0:T(8,128)(2,1)S(1)} %get-tuple-element.42), channel_id=1, source_target_pairs={{0,28},{2,30},{4,0},{6,2},{8,4},{10,6},{12,8},{14,10},{16,12},{18,... | collective-permute-start | bytes 196616 | tf_op jit(solution)/shard_map/ppermute | solution.py:98
  687.5 10.9 %collective-permute-start.17 = (bf16[1,8,4096]{2,1,0:T(8,128)(2,1)S(1)}, bf16[1,8,4096]{2,1,0:T(8,128)(2,1)S(1)}, u32[]{:S(2)}, u32[]{:S(2)}) collective-permute-start(bf16[1,8,4096]{2,1,0:T(8,128)(2,1)S(1)} %get-tuple-element.41), channel_id=1, source_target_pairs={{0,26},{2,28},{4,30},{6,0},{8,2},{10,4},{12,6},{14,8},{16,10},{18,... | collective-permute-start | bytes 196616 | tf_op jit(solution)/shard_map/ppermute | solution.py:98
  689.0 10.4 %collective-permute-start.18 = (bf16[1,8,4096]{2,1,0:T(8,128)(2,1)S(1)}, bf16[1,8,4096]{2,1,0:T(8,128)(2,1)S(1)}, u32[]{:S(2)}, u32[]{:S(2)}) collective-permute-start(bf16[1,8,4096]{2,1,0:T(8,128)(2,1)S(1)} %get-tuple-element.40), channel_id=1, source_target_pairs={{0,24},{2,26},{4,28},{6,30},{8,0},{10,2},{12,4},{14,6},{16,8},{18,... | collective-permute-start | bytes 196616 | tf_op jit(solution)/shard_map/ppermute | solution.py:98
  696.8 10.5 %collective-permute-start.21 = (bf16[1,8,4096]{2,1,0:T(8,128)(2,1)S(1)}, bf16[1,8,4096]{2,1,0:T(8,128)(2,1)S(1)}, u32[]{:S(2)}, u32[]{:S(2)}) collective-permute-start(bf16[1,8,4096]{2,1,0:T(8,128)(2,1)S(1)} %get-tuple-element.37), channel_id=1, source_target_pairs={{0,18},{2,20},{4,22},{6,24},{8,26},{10,28},{12,30},{14,0},{16,2},{... | collective-permute-start | bytes 196616 | tf_op jit(solution)/shard_map/ppermute | solution.py:98
  698.3 13.0 %collective-permute-start.22 = (bf16[1,8,4096]{2,1,0:T(8,128)(2,1)S(1)}, bf16[1,8,4096]{2,1,0:T(8,128)(2,1)S(1)}, u32[]{:S(2)}, u32[]{:S(2)}) collective-permute-start(bf16[1,8,4096]{2,1,0:T(8,128)(2,1)S(1)} %get-tuple-element.36), channel_id=1, source_target_pairs={{0,16},{2,18},{4,20},{6,22},{8,24},{10,26},{12,28},{14,30},{16,0},... | collective-permute-start | bytes 196616 | tf_op jit(solution)/shard_map/ppermute | solution.py:98
  699.4 12.0 %collective-permute-start.23 = (bf16[1,8,4096]{2,1,0:T(8,128)(2,1)S(1)}, bf16[1,8,4096]{2,1,0:T(8,128)(2,1)S(1)}, u32[]{:S(2)}, u32[]{:S(2)}) collective-permute-start(bf16[1,8,4096]{2,1,0:T(8,128)(2,1)S(1)} %get-tuple-element.35), channel_id=1, source_target_pairs={{0,14},{2,16},{4,18},{6,20},{8,22},{10,24},{12,26},{14,28},{16,30}... | collective-permute-start | bytes 196616 | tf_op jit(solution)/shard_map/ppermute | solution.py:98
  702.6 13.7 %collective-permute-start.24 = (bf16[1,8,4096]{2,1,0:T(8,128)(2,1)S(1)}, bf16[1,8,4096]{2,1,0:T(8,128)(2,1)S(1)}, u32[]{:S(2)}, u32[]{:S(2)}) collective-permute-start(bf16[1,8,4096]{2,1,0:T(8,128)(2,1)S(1)} %get-tuple-element.34), channel_id=1, source_target_pairs={{0,12},{2,14},{4,16},{6,18},{8,20},{10,22},{12,24},{14,26},{16,28}... | collective-permute-start | bytes 196616 | tf_op jit(solution)/shard_map/ppermute | solution.py:98
  703.6 12.8 %collective-permute-start.25 = (bf16[1,8,4096]{2,1,0:T(8,128)(2,1)S(1)}, bf16[1,8,4096]{2,1,0:T(8,128)(2,1)S(1)}, u32[]{:S(2)}, u32[]{:S(2)}) collective-permute-start(bf16[1,8,4096]{2,1,0:T(8,128)(2,1)S(1)} %get-tuple-element.33), channel_id=1, source_target_pairs={{0,10},{2,12},{4,14},{6,16},{8,18},{10,20},{12,22},{14,24},{16,26}... | collective-permute-start | bytes 196616 | tf_op jit(solution)/shard_map/ppermute | solution.py:98
  707.3 9.1 %collective-permute-start.26 = (bf16[1,8,4096]{2,1,0:T(8,128)(2,1)S(1)}, bf16[1,8,4096]{2,1,0:T(8,128)(2,1)S(1)}, u32[]{:S(2)}, u32[]{:S(2)}) collective-permute-start(bf16[1,8,4096]{2,1,0:T(8,128)(2,1)S(1)} %get-tuple-element.32), channel_id=1, source_target_pairs={{0,8},{2,10},{4,12},{6,14},{8,16},{10,18},{12,20},{14,22},{16,24},... | collective-permute-start | bytes 196616 | tf_op jit(solution)/shard_map/ppermute | solution.py:98
  (19 other events, 468.6 us)
Sparse Core Ops, SparseCore 0:
  136.2 13.4 all-gather.2
  248.6 12.0 all-gather.4
  267.9 12.7 reduce-scatter.2
  283.4 12.1 reduce-scatter.4
